TPU v7x, 256 devices: a whole 4x4x8 slice. The times are simulated.
256 devices in a mesh: row: 8 (over x, core), col: 32 (over z, y).
Axes of the slice: x: 4, y: 4, z: 8, core: 2. Of those that a mesh axis runs over, the one named last changes fastest.
Arguments:
- inputs: bfloat16 [1024, 8192], P('col', 'row'), may hold values from -6 to 6
- target: bfloat16 [1024, 8192], P(None, 'row'), may hold values from -6 to 6
- gate_weight: bfloat16 [8192, 16384], P('row', 'col'), may hold values from -0.0625 to 0.0625
- up_weight: bfloat16 [8192, 16384], P('row', 'col'), may hold values from -0.0625 to 0.0625
- down_weight: bfloat16 [16384, 8192], P('col', 'row'), may hold values from -0.046875 to 0.046875
Outputs:
- output: bfloat16 [1024, 8192], P('col', 'row')
- grad_inputs: bfloat16 [1024, 8192], P('col', 'row')
- grad_gate_weight: bfloat16 [8192, 16384], P('row', 'col')
- grad_up_weight: bfloat16 [8192, 16384], P('row', 'col')
- grad_down_weight: bfloat16 [16384, 8192], P('col', 'row')
All inputs are finite; a program needn't handle non-finite values.
Results may differ from a plain program's by a relative error of at most 0.0065.
Values may be sent and summed in bfloat16 or wider, within the bound.
No kernel may reach another device: no remote copies, remote signals or barrier semaphores. Data moves between devices by JAX's collectives and lax.ppermute only.
A program may use at most 64 MiB of HBM per device.

v0:
```python
import jax
import jax.numpy as jnp
from jax import lax
from jax.sharding import Mesh, PartitionSpec as P

F32 = jnp.float32
BF16 = jnp.bfloat16
NX, NC, NZ, NY = (4, 2, 8, 4)


def contract_first(left, right):
    return lax.dot_general(left, right, (((0,), (0,)), ((), ())), preferred_element_type=F32)


def contract_last(left, right):
    return lax.dot_general(left, right, (((1,), (1,)), ((), ())), preferred_element_type=F32)


def exchange(val, axis):
    return lax.all_to_all(val, axis, split_axis=0, concat_axis=0, tiled=True)


def scatter_sum(part, axis, size):
    rows, cols = part.shape
    got = exchange(part.astype(BF16), axis).reshape(size, rows // size, cols)
    return jnp.sum(got.astype(F32), axis=0)


def spread(own, axis, size):
    rows, cols = own.shape
    return exchange(
        jnp.broadcast_to(own[None], (size, rows, cols)).reshape(size * rows, cols), axis
    )


def gather_col(own):
    return lax.all_gather(spread(own, "z", NZ), "y", axis=0, tiled=True)


def scatter_col(part):
    return scatter_sum(scatter_sum(part, "y", NY), "z", NZ)


def swap_core(val):
    return lax.ppermute(val, "core", [(0, 1), (1, 0)])


def scatter_row(part):
    half = part.shape[0] // NC
    core = lax.axis_index("core")
    mine = lax.dynamic_slice_in_dim(part, core * half, half, 0)
    other = lax.dynamic_slice_in_dim(part, (1 - core) * half, half, 0)
    both = mine + swap_core(other.astype(BF16)).astype(F32)
    return scatter_sum(both, "x", NX)


def gather_row(own):
    mine = spread(own, "x", NX)
    other = swap_core(mine)
    first = lax.axis_index("core") == 0
    return jnp.concatenate([jnp.where(first, mine, other), jnp.where(first, other, mine)], axis=0)


def gate_grads(hidden_grad, gate_act, up_act):
    sigma = jax.nn.sigmoid(gate_act)
    silu_val = gate_act * sigma
    grad_gate = hidden_grad * up_act * sigma * (1.0 + gate_act * (1.0 - sigma))
    grad_up = hidden_grad * silu_val
    return jnp.concatenate([grad_gate.astype(BF16), grad_up.astype(BF16)], axis=1)


def body(inputs, target, gate_weight, up_weight, down_weight):
    wide = gate_weight.shape[1]
    tok_own = inputs.shape[0]
    tokens_all = gather_col(inputs)
    gate_part = jnp.dot(tokens_all, gate_weight, preferred_element_type=F32)
    up_part = jnp.dot(tokens_all, up_weight, preferred_element_type=F32)
    acts = scatter_row(jnp.concatenate([gate_part, up_part], axis=1))
    gate_own, up_own = (acts[:, :wide], acts[:, wide:])
    hidden_own = (jax.nn.silu(gate_own) * up_own).astype(BF16)
    hidden_all = gather_row(hidden_own)
    result_part = jnp.dot(hidden_all, down_weight, preferred_element_type=F32)
    result_own = scatter_col(result_part)
    offset = (lax.axis_index("z") * NY + lax.axis_index("y")) * tok_own
    target_own = lax.dynamic_slice_in_dim(target, offset, tok_own, 0)
    error_own = (result_own - target_own.astype(F32)).astype(BF16)
    output = result_own.astype(BF16)
    error_all = gather_col(error_own)
    hidden_grad = scatter_row(contract_last(error_all, down_weight))
    grads_all = gather_row(gate_grads(hidden_grad, gate_own, up_own))
    gate_grad_all, up_grad_all = (grads_all[:, :wide], grads_all[:, wide:])
    input_grad_part = contract_last(gate_grad_all, gate_weight) + contract_last(
        up_grad_all, up_weight
    )
    grad_inputs = scatter_col(input_grad_part).astype(BF16)
    grad_down_weight = contract_first(hidden_all, error_all).astype(BF16)
    grad_gate_weight = contract_first(tokens_all, gate_grad_all).astype(BF16)
    grad_up_weight = contract_first(tokens_all, up_grad_all).astype(BF16)
    return (output, grad_inputs, grad_gate_weight, grad_up_weight, grad_down_weight)


def solution(mesh):
    fine = Mesh(mesh.devices.reshape(NX, NC, NZ, NY), ("x", "core", "z", "y"))
    row, col = (("x", "core"), ("z", "y"))
    placed = (P(col, row), P(None, row), P(row, col), P(row, col), P(col, row))
    return jax.shard_map(
        body,
        mesh=fine,
        in_specs=placed,
        out_specs=(P(col, row), P(col, row), P(row, col), P(row, col), P(col, row)),
        check_vma=False,
    )
```

profile of v0, /device:TPU:1, one launch (start us, length us, event | category | flops | bytes accessed | tf_op | source)
XLA Modules:
  0.0 317.7 jit_solution(8181957383931177860)
XLA Ops:
  7.2 1.0 broadcast_in_dim.8
  8.2 25.0 %all_to_all.90 = bf16[8,32,1024]{2,1,0:T(8,128)(2,1)} all-to-all(bf16[8,32,1024]{2,1,0:T(8,128)(2,1)S(1)} %broadcast_in_dim.8), channel_id=1, replica_groups=mesh['x'=4,'core'=2,'z'=8,'y'=4] {'z'}, dimensions={0} | all-to-all | bytes 1048576 | tf_op jit(solution)/shard_map/all_to_all | solution.py:20
  33.3 31.3 %all-gather.3.cloned.1.call-done = bf16[1024,1024]{1,0:T(8,128)(2,1)} async-done(((bf16[256,1024]{1,0:T(8,128)(2,1)}), bf16[1024,1024]{1,0:T(8,128)(2,1)}) %all-gather.3.cloned.1.call-update) | async-done | bytes 2097168 | tf_op jit(solution)/shard_map/all_gather | solution.py:37
  64.6 3.3 %fusion.18 = f32[1024,512]{0,1:T(8,128)S(1)} fusion(bf16[1024,1024]{1,0:T(8,128)(2,1)} %all-gather.3.cloned.1.call-done, bf16[1024,512]{1,0:T(8,128)(2,1)} %param.8), kind=kOutput, calls=%fused_computation.45 | convolution fusion | flops 1073741824 | bytes 5242880 | tf_op jit(solution)/shard_map/dot_general | solution.py:77
  67.9 1.3 fusion.17
  69.2 1.3 fusion.1
  70.5 0.4 copy-done.1
  70.9 0.8 collective-permute-start
  71.8 2.6 collective-permute-done
  74.4 1.7 copy_bitcast_fusion
  76.2 18.0 %all_to_all.91 = bf16[4,128,1024]{1,2,0:T(8,128)(2,1)S(1)} all-to-all(bf16[4,128,1024]{1,2,0:T(8,128)(2,1)S(1)} %copy_bitcast_fusion), channel_id=1, replica_groups=mesh['x'=4,'core'=2,'z'=8,'y'=4] {'x'}, dimensions={0} | all-to-all | bytes 2097152 | tf_op jit(solution)/shard_map/all_to_all | solution.py:20
  94.2 0.1 convert_reduce_fusion
  94.3 0.8 copy-done.2
  95.4 10.2 %all_to_all.92 = bf16[4,128,512]{2,1,0:T(8,128)(2,1)S(1)} all-to-all(bf16[4,128,512]{2,1,0:T(8,128)(2,1)S(1)} %broadcast_in_dim.9), channel_id=1, replica_groups=mesh['x'=4,'core'=2,'z'=8,'y'=4] {'x'}, dimensions={0} | all-to-all | bytes 1048576 | tf_op jit(solution)/shard_map/all_to_all | solution.py:20
  105.5 2.7 collective-permute-start.1
  108.2 1.5 collective-permute-done.1
  109.9 1.3 convolution_convert_fusion
  111.2 28.0 %all_to_all.93 = bf16[4,256,1024]{2,1,0:T(8,128)(2,1)S(1)} all-to-all(bf16[4,256,1024]{2,1,0:T(8,128)(2,1)S(1)} %bitcast.38), channel_id=1, replica_groups=mesh['x'=4,'core'=2,'z'=8,'y'=4] {'y'}, dimensions={0} | all-to-all | bytes 4194304 | tf_op jit(solution)/shard_map/all_to_all | solution.py:20
  139.2 1.3 reduce_sum.64
  140.5 6.7 %all-to-all-start.4 = ((bf16[8,32,1024]{2,1,0:T(8,128)(2,1)}), bf16[8,32,1024]{2,1,0:T(8,128)(2,1)S(1)}, u32[]{:S(2)}, u32[]{:S(2)}) async-start(bf16[8,32,1024]{2,1,0:T(8,128)(2,1)} %bitcast.41), calls=%async_computation.4 | async-start | bytes 1048576 | tf_op jit(solution)/shard_map/all_to_all | solution.py:20
  147.3 15.7 %all-to-all-done.4 = bf16[8,32,1024]{2,1,0:T(8,128)(2,1)S(1)} async-done(((bf16[8,32,1024]{2,1,0:T(8,128)(2,1)}), bf16[8,32,1024]{2,1,0:T(8,128)(2,1)S(1)}, u32[]{:S(2)}, u32[]{:S(2)}) %all-to-all-start.4) | async-done | bytes 524320 | tf_op jit(solution)/shard_map/all_to_all | solution.py:20
  163.0 1.5 subtract_convert_fusion
  164.6 17.5 %all_to_all.94 = bf16[8,32,1024]{2,1,0:T(8,128)(2,1)} all-to-all(bf16[8,32,1024]{2,1,0:T(8,128)(2,1)S(1)} %broadcast_in_dim.10), channel_id=1, replica_groups=mesh['x'=4,'core'=2,'z'=8,'y'=4] {'z'}, dimensions={0} | all-to-all | bytes 1048576 | tf_op jit(solution)/shard_map/all_to_all | solution.py:20
  182.2 29.1 %all-gather.5.cloned.1.call-done = bf16[1024,1024]{1,0:T(8,128)(2,1)} async-done(((bf16[256,1024]{1,0:T(8,128)(2,1)}), bf16[1024,1024]{1,0:T(8,128)(2,1)}) %all-gather.5.cloned.1.call-update) | async-done | bytes 2097168 | tf_op jit(solution)/shard_map/all_gather | solution.py:37
  211.3 2.9 fusion.19
  214.2 0.9 collective-permute-start.2
  215.2 1.5 collective-permute-done.2
  216.7 0.2 add_convert_fusion.1
  216.9 12.4 %all_to_all.95 = bf16[4,128,512]{2,1,0:T(8,128)(2,1)S(1)} all-to-all(bf16[4,128,512]{2,1,0:T(8,128)(2,1)S(1)} %bitcast.37), channel_id=1, replica_groups=mesh['x'=4,'core'=2,'z'=8,'y'=4] {'x'}, dimensions={0} | all-to-all | bytes 1048576 | tf_op jit(solution)/shard_map/all_to_all | solution.py:20
  229.4 0.1 copy.29
  229.5 0.2 multiply_convert_fusion.1
  229.7 0.1 copy.31
  230.0 15.8 %all_to_all.96 = bf16[4,128,1024]{2,1,0:T(8,128)(2,1)S(1)} all-to-all(bf16[4,128,1024]{2,1,0:T(8,128)(2,1)S(1)} %broadcast_in_dim.11), channel_id=1, replica_groups=mesh['x'=4,'core'=2,'z'=8,'y'=4] {'x'}, dimensions={0} | all-to-all | bytes 2097152 | tf_op jit(solution)/shard_map/all_to_all | solution.py:20
  245.8 2.7 collective-permute-start.3
  248.5 2.3 collective-permute-done.3
  250.7 0.2 broadcast_select_fusion.1
  251.0 1.3 fusion.10
  252.3 1.3 add_convert_fusion
  253.6 29.3 %all_to_all.97 = bf16[4,256,1024]{2,1,0:T(8,128)(2,1)} all-to-all(bf16[4,256,1024]{2,1,0:T(8,128)(2,1)S(1)} %bitcast.34), channel_id=1, replica_groups=mesh['x'=4,'core'=2,'z'=8,'y'=4] {'y'}, dimensions={0} | all-to-all | bytes 4194304 | tf_op jit(solution)/shard_map/all_to_all | solution.py:20
  282.8 2.9 reduce_sum.67
  285.8 6.7 %all-to-all-start.9 = ((bf16[8,32,1024]{2,1,0:T(8,128)(2,1)}), bf16[8,32,1024]{2,1,0:T(8,128)(2,1)}, u32[]{:S(2)}, u32[]{:S(2)}) async-start(bf16[8,32,1024]{2,1,0:T(8,128)(2,1)} %bitcast.42), calls=%async_computation.9 | async-start | bytes 1048576 | tf_op jit(solution)/shard_map/all_to_all | solution.py:20
  292.5 4.3 %convolution_convert_fusion.1 = bf16[512,1024]{1,0:T(8,128)(2,1)} fusion(bf16[1024,1024]{1,0:T(8,128)(2,1)} %all-gather.5.cloned.1.call-done, bf16[512,512]{1,0:T(8,128)(2,1)} %copy-done.10, bf16[512,512]{1,0:T(8,128)(2,1)} %copy-done.9), kind=kOutput, calls=%fused_computation.14 | convolution fusion | flops 1076363264 | bytes 4194304 | tf_op jit(solution)/shard_map/dot_general | solution.py:12
  296.8 2.2 fusion.6
  299.1 2.3 copy.33
  301.4 3.9 %fusion.5 = bf16[1024,512]{0,1:T(8,128)(2,1)} fusion(bf16[1024,1024]{1,0:T(8,128)(2,1)} %all-gather.3.cloned.1.call-done, bf16[512,1024]{1,0:T(8,128)(2,1)S(1)} %get-tuple-element.25, bf16[512,1024]{1,0:T(8,128)(2,1)S(1)} %get-tuple-element.26), kind=kOutput, calls=%fused_computation.17 | convolution fusion | flops 1076363264 | bytes 5242880 | tf_op jit(solution)/shard_map/dot_general | solution.py:12
  305.2 2.3 copy.32
  307.5 1.6 all-to-all-done.9
  309.1 1.8 reduce_sum.68
  (34 shorter events, 0.9 us)
Async XLA Ops:
  7.2 102.7 %copy-start = (bf16[512,1024]{1,0:T(8,128)(2,1)S(1)}, bf16[512,1024]{1,0:T(8,128)(2,1)}, u32[]{:S(2)}) copy-start(bf16[512,1024]{1,0:T(8,128)(2,1)} %param.9) | copy-start | bytes 3145732
  7.2 57.4 %all-gather.3.cloned.1.call-start = ((), (), s32[]{:S(2)}) async-start(), calls=%async_computation.10 | async-start | bytes 2621440 | tf_op jit(solution)/shard_map/all_gather | solution.py:37
  64.6 3.3 %copy-start.4 = (bf16[1024,1024]{1,0:T(8,128)(2,1)S(1)}, bf16[1024,1024]{1,0:T(8,128)(2,1)}, u32[]{:S(2)}) copy-start(bf16[1024,1024]{1,0:T(8,128)(2,1)} %all-gather.3.cloned.1.call-done) | copy-start | bytes 6291460
  64.6 3.3 %copy-start.7 = (bf16[1024,512]{1,0:T(8,128)(2,1)S(1)}, bf16[1024,512]{1,0:T(8,128)(2,1)}, u32[]{:S(2)}) copy-start(bf16[1024,512]{1,0:T(8,128)(2,1)} %param.7) | copy-start | bytes 3145732
  69.2 1.7 copy-start.1
  70.9 3.5 %collective-permute-start = (bf16[512,1024]{0,1:T(8,128)(2,1)}, bf16[512,1024]{0,1:T(8,128)(2,1)}, u32[]{:S(2)}, u32[]{:S(2)}) collective-permute-start(bf16[512,1024]{0,1:T(8,128)(2,1)} %fusion.1), channel_id=1, source_target_pairs={{0,32},{32,0},{1,33},{33,1},{2,34},{34,2},{3,35},{35,3},{4,36},{36... | collective-permute-start | bytes 3145736 | tf_op jit(solution)/shard_map/ppermute | solution.py:45
  94.3 0.8 copy-start.2
  105.5 4.2 %collective-permute-start.1 = (bf16[512,512]{1,0:T(8,128)(2,1)S(1)}, bf16[512,512]{1,0:T(8,128)(2,1)S(1)}, u32[]{:S(2)}, u32[]{:S(2)}) collective-permute-start(bf16[512,512]{1,0:T(8,128)(2,1)S(1)} %bitcast.36), channel_id=1, source_target_pairs={{0,32},{32,0},{1,33},{33,1},{2,34},{34,2},{3,35},{35,3},{4,36},{36... | collective-permute-start | bytes 1572872 | tf_op jit(solution)/shard_map/ppermute | solution.py:45
  109.8 1.3 copy-start.9
  109.9 1.3 copy-start.10
  140.5 22.5 %all-to-all-start.4 = ((bf16[8,32,1024]{2,1,0:T(8,128)(2,1)}), bf16[8,32,1024]{2,1,0:T(8,128)(2,1)S(1)}, u32[]{:S(2)}, u32[]{:S(2)}) async-start(bf16[8,32,1024]{2,1,0:T(8,128)(2,1)} %bitcast.41), calls=%async_computation.4 | async-start | bytes 1048576 | tf_op jit(solution)/shard_map/all_to_all | solution.py:20
  147.2 64.1 %all-gather.5.cloned.1.call-start = ((), (), s32[]{:S(2)}) async-start(), calls=%async_computation.11 | async-start | bytes 2621440 | tf_op jit(solution)/shard_map/all_gather | solution.py:37
  214.2 15.3 %copy-start.3 = (f32[128,1024]{0,1:T(8,128)S(1)}, f32[128,1024]{0,1:T(8,128)}, u32[]{:S(2)}) copy-start(f32[128,1024]{0,1:T(8,128)} %copy-done.2) | copy-start | bytes 1572868
  214.2 2.5 collective-permute-start.2
  245.8 5.2 %copy-start.6 = (bf16[1024,512]{1,0:T(8,128)(2,1)S(1)}, bf16[1024,512]{1,0:T(8,128)(2,1)}, u32[]{:S(2)}) copy-start(bf16[1024,512]{1,0:T(8,128)(2,1)} %param.8) | copy-start | bytes 3145732
  245.8 4.9 %collective-permute-start.3 = (bf16[512,1024]{1,0:T(8,128)(2,1)S(1)}, bf16[512,1024]{1,0:T(8,128)(2,1)S(1)}, u32[]{:S(2)}, u32[]{:S(2)}) collective-permute-start(bf16[512,1024]{1,0:T(8,128)(2,1)S(1)} %bitcast.35), channel_id=1, source_target_pairs={{0,32},{32,0},{1,33},{33,1},{2,34},{34,2},{3,35},{35,3},{4,36},{36... | collective-permute-start | bytes 3145736 | tf_op jit(solution)/shard_map/ppermute | solution.py:45
  251.0 1.3 copy-start.8
  285.8 23.3 %all-to-all-start.9 = ((bf16[8,32,1024]{2,1,0:T(8,128)(2,1)}), bf16[8,32,1024]{2,1,0:T(8,128)(2,1)}, u32[]{:S(2)}, u32[]{:S(2)}) async-start(bf16[8,32,1024]{2,1,0:T(8,128)(2,1)} %bitcast.42), calls=%async_computation.9 | async-start | bytes 1048576 | tf_op jit(solution)/shard_map/all_to_all | solution.py:20
  292.5 4.3 %copy-start.5 = (bf16[1024,1024]{1,0:T(8,128)(2,1)S(1)}, bf16[1024,1024]{1,0:T(8,128)(2,1)}, u32[]{:S(2)}) copy-start(bf16[1024,1024]{1,0:T(8,128)(2,1)} %all-gather.3.cloned.1.call-done) | copy-start | bytes 6291460
Sparse Core Ops, SparseCore 0:
  33.4 31.1 all-gather.2
  182.3 28.9 all-gather.4
where the time goes:
time: 319 us; the launch traced here: 318 us
  blocking collectives  156 us (49%)
  waiting for transfers between devices  85.8 us (27%)
  matrix products  21.7 us (7%)
  starting transfers between devices  20.7 us (6%)
  between operations  14.3 us (4%)
  other arithmetic  11.6 us (4%)
  local copies, waits for them, and re-layouts  7.41 us (2%)
    all_to_all x8, blocking collectives, exchange(): return lax.all_to_all(val, axis, split_axis=0, concat_axis=0, tiled=True)  156 us
    all_gather x2, waiting for transfers between devices, gather_col(): return lax.all_gather(spread(own, 'z', NZ), 'y', axis=0, tiled=True)  60.5 us
    all_to_all x2, waiting for transfers between devices, exchange(): return lax.all_to_all(val, axis, split_axis=0, concat_axis=0, tiled=True)  17.3 us
    all_to_all x2, starting transfers between devices, exchange(): return lax.all_to_all(val, axis, split_axis=0, concat_axis=0, tiled=True)  13.5 us
    dot_general x3, matrix products, contract_first(): lax.dot_general(left, right, (((0,), (0,)), ((), ())), preferred_element_...  10.4 us
    ppermute x4, waiting for transfers between devices, swap_core(): return lax.ppermute(val, 'core', [(0, 1), (1, 0)])  7.99 us
    ppermute x4, starting transfers between devices, swap_core(): return lax.ppermute(val, 'core', [(0, 1), (1, 0)])  7.1 us
  transfers between devices with their start and end apart: 8, of which 8 were waited for; matrix products, arithmetic and copies ran while one was open for 5% of the time, Pallas kernels for 0%

commit v1 on v0

--- a/solution.py
+++ b/solution.py
@@ -34,7 +34,9 @@
 
 
 def gather_col(own):
-    return lax.all_gather(spread(own, "z", NZ), "y", axis=0, tiled=True)
+    return jnp.concatenate(
+        lax.all_to_all(jnp.stack([spread(own, "z", NZ)] * lax.axis_size("y")), "y", 0, 0), axis=0
+    )
 
 
 def scatter_col(part):

time: 319 us -> 302 us (0.947)
  waiting for transfers between devices: 85.8 us -> 50.8 us
  blocking collectives: 156 us -> 183 us
  between operations: 14.3 us -> 0.95 us
  starting transfers between devices: 20.7 us -> 24 us
    all_gather x2 -> x0, waiting for transfers between devices: 60.5 us -> none  [gather_col(): return lax.all_gather(spread(own, 'z', NZ), 'y', axis=0, tiled=True)]
    all_to_all x0 -> x1, blocking collectives: none -> 25.9 us  [gather_col(): lax.all_to_all(jnp.stack([spread(own, 'z', NZ)] * lax.axis_size('y')), 'y...]
    all_to_all x0 -> x1, waiting for transfers between devices: none -> 23.8 us  [gather_col(): lax.all_to_all(jnp.stack([spread(own, 'z', NZ)] * lax.axis_size('y')), 'y...]
    all_to_all x2, starting transfers between devices: 13.5 us -> 7.63 us  [exchange(): return lax.all_to_all(val, axis, split_axis=0, concat_axis=0, tiled=True)]
    ppermute x4, starting transfers between devices: 7.1 us -> 12.2 us  [swap_core(): return lax.ppermute(val, 'core', [(0, 1), (1, 0)])]
    all_to_all x0 -> x1, starting transfers between devices: none -> 4.18 us  [gather_col(): lax.all_to_all(jnp.stack([spread(own, 'z', NZ)] * lax.axis_size('y')), 'y...]
    unnamed x24 -> x28, local copies, waits for them, and re-layouts: 5.78 us -> 7.07 us
  transfers between devices with their start and end apart: 8 -> 7, of which waited for: 8 -> 7; matrix products, arithmetic and copies ran while one was open for 5% -> 5% of each run, Pallas kernels for 0% -> 0%
where the time goes in v1:
time: 302 us; the launch traced here: 301 us
  blocking collectives  183 us (61%)
  waiting for transfers between devices  50.8 us (17%)
  starting transfers between devices  24 us (8%)
  matrix products  20.1 us (7%)
  other arithmetic  11.6 us (4%)
  local copies, waits for them, and re-layouts  10.6 us (4%)
    all_to_all x8, blocking collectives, exchange(): return lax.all_to_all(val, axis, split_axis=0, concat_axis=0, tiled=True)  157 us
    all_to_all x1, blocking collectives, gather_col(): lax.all_to_all(jnp.stack([spread(own, 'z', NZ)] * lax.axis_size('y')), 'y...  25.9 us
    all_to_all x1, waiting for transfers between devices, gather_col(): lax.all_to_all(jnp.stack([spread(own, 'z', NZ)] * lax.axis_size('y')), 'y...  23.8 us
    all_to_all x2, waiting for transfers between devices, exchange(): return lax.all_to_all(val, axis, split_axis=0, concat_axis=0, tiled=True)  19 us
    ppermute x4, starting transfers between devices, swap_core(): return lax.ppermute(val, 'core', [(0, 1), (1, 0)])  12.2 us
    dot_general x3, matrix products, contract_first(): lax.dot_general(left, right, (((0,), (0,)), ((), ())), preferred_element_...  10.4 us
    ppermute x4, waiting for transfers between devices, swap_core(): return lax.ppermute(val, 'core', [(0, 1), (1, 0)])  7.99 us
    all_to_all x2, starting transfers between devices, exchange(): return lax.all_to_all(val, axis, split_axis=0, concat_axis=0, tiled=True)  7.63 us
  transfers between devices with their start and end apart: 7, of which 7 were waited for; matrix products, arithmetic and copies ran while one was open for 5% of the time, Pallas kernels for 0%

profile of v1, /device:TPU:1, one launch (start us, length us, event | category | flops | bytes accessed | tf_op | source)
XLA Modules:
  0.0 301.0 jit_solution(4285362848797881154)
XLA Ops:
  0.6 1.0 broadcast_in_dim.8
  1.6 24.9 %all_to_all.94 = bf16[8,32,1024]{2,1,0:T(8,128)(2,1)S(1)} all-to-all(bf16[8,32,1024]{2,1,0:T(8,128)(2,1)S(1)} %broadcast_in_dim.8), channel_id=1, replica_groups=mesh['x'=4,'core'=2,'z'=8,'y'=4] {'z'}, dimensions={0} | all-to-all | bytes 1048576 | tf_op jit(solution)/shard_map/all_to_all | solution.py:20
  26.5 1.6 stack.9
  28.2 4.2 %all-to-all-start.1 = ((bf16[4,256,1024]{2,1,0:T(8,128)(2,1)}), bf16[4,256,1024]{2,1,0:T(8,128)(2,1)S(1)}, u32[]{:S(2)}, u32[]{:S(2)}) async-start(bf16[4,256,1024]{2,1,0:T(8,128)(2,1)} %stack.9), calls=%async_computation.1 | async-start | bytes 4194304 | tf_op jit(solution)/shard_map/all_to_all | solution.py:38
  32.4 23.8 %all-to-all-done.1 = bf16[4,256,1024]{2,1,0:T(8,128)(2,1)S(1)} async-done(((bf16[4,256,1024]{2,1,0:T(8,128)(2,1)}), bf16[4,256,1024]{2,1,0:T(8,128)(2,1)S(1)}, u32[]{:S(2)}, u32[]{:S(2)}) %all-to-all-start.1) | async-done | bytes 2097184 | tf_op jit(solution)/shard_map/all_to_all | solution.py:38
  56.2 1.3 copy-done.2
  57.5 3.3 %fusion.18 = f32[1024,512]{0,1:T(8,128)S(1)} fusion(bf16[1024,1024]{1,0:T(8,128)(2,1)} %bitcast.36, bf16[1024,512]{1,0:T(8,128)(2,1)} %param.8), kind=kOutput, calls=%fused_computation.45 | convolution fusion | flops 1073741824 | bytes 5242880 | tf_op jit(solution)/shard_map/dot_general | solution.py:79
  60.8 1.3 fusion.17
  62.2 1.3 fusion.1
  63.4 0.3 copy-done.1
  63.8 3.5 %collective-permute-start = (bf16[512,1024]{0,1:T(8,128)(2,1)}, bf16[512,1024]{0,1:T(8,128)(2,1)}, u32[]{:S(2)}, u32[]{:S(2)}) collective-permute-start(bf16[512,1024]{0,1:T(8,128)(2,1)} %fusion.1), channel_id=1, source_target_pairs={{0,32},{32,0},{1,33},{33,1},{2,34},{34,2},{3,35},{35,3},{4,36},{36... | collective-permute-start | bytes 3145736 | tf_op jit(solution)/shard_map/ppermute | solution.py:47
  67.3 2.6 collective-permute-done
  69.9 1.7 copy_bitcast_fusion
  71.6 18.1 %all_to_all.95 = bf16[4,128,1024]{1,2,0:T(8,128)(2,1)S(1)} all-to-all(bf16[4,128,1024]{1,2,0:T(8,128)(2,1)S(1)} %copy_bitcast_fusion), channel_id=1, replica_groups=mesh['x'=4,'core'=2,'z'=8,'y'=4] {'x'}, dimensions={0} | all-to-all | bytes 2097152 | tf_op jit(solution)/shard_map/all_to_all | solution.py:20
  89.8 0.8 copy-done.5
  90.9 10.2 %all_to_all.96 = bf16[4,128,512]{2,1,0:T(8,128)(2,1)S(1)} all-to-all(bf16[4,128,512]{2,1,0:T(8,128)(2,1)S(1)} %broadcast_in_dim.9), channel_id=1, replica_groups=mesh['x'=4,'core'=2,'z'=8,'y'=4] {'x'}, dimensions={0} | all-to-all | bytes 1048576 | tf_op jit(solution)/shard_map/all_to_all | solution.py:20
  101.0 2.7 collective-permute-start.1
  103.7 1.5 collective-permute-done.1
  105.4 1.3 convolution_convert_fusion
  106.7 28.5 %all_to_all.97 = bf16[4,256,1024]{2,1,0:T(8,128)(2,1)S(1)} all-to-all(bf16[4,256,1024]{2,1,0:T(8,128)(2,1)S(1)} %bitcast.48), channel_id=1, replica_groups=mesh['x'=4,'core'=2,'z'=8,'y'=4] {'y'}, dimensions={0} | all-to-all | bytes 4194304 | tf_op jit(solution)/shard_map/all_to_all | solution.py:20
  135.2 1.3 reduce_sum.64
  136.5 3.5 %all-to-all-start.5 = ((bf16[8,32,1024]{2,1,0:T(8,128)(2,1)}), bf16[8,32,1024]{2,1,0:T(8,128)(2,1)S(1)}, u32[]{:S(2)}, u32[]{:S(2)}) async-start(bf16[8,32,1024]{2,1,0:T(8,128)(2,1)} %bitcast.49), calls=%async_computation.5 | async-start | bytes 1048576 | tf_op jit(solution)/shard_map/all_to_all | solution.py:20
  140.0 16.9 %all-to-all-done.5 = bf16[8,32,1024]{2,1,0:T(8,128)(2,1)S(1)} async-done(((bf16[8,32,1024]{2,1,0:T(8,128)(2,1)}), bf16[8,32,1024]{2,1,0:T(8,128)(2,1)S(1)}, u32[]{:S(2)}, u32[]{:S(2)}) %all-to-all-start.5) | async-done | bytes 524320 | tf_op jit(solution)/shard_map/all_to_all | solution.py:20
  157.0 1.5 subtract_convert_fusion
  158.6 18.1 %all_to_all.98 = bf16[8,32,1024]{2,1,0:T(8,128)(2,1)S(1)} all-to-all(bf16[8,32,1024]{2,1,0:T(8,128)(2,1)S(1)} %broadcast_in_dim.10), channel_id=1, replica_groups=mesh['x'=4,'core'=2,'z'=8,'y'=4] {'z'}, dimensions={0} | all-to-all | bytes 1048576 | tf_op jit(solution)/shard_map/all_to_all | solution.py:20
  176.7 0.3 stack.21
  176.9 25.9 %all_to_all.99 = bf16[4,256,1024]{2,1,0:T(8,128)(2,1)S(1)} all-to-all(bf16[4,256,1024]{2,1,0:T(8,128)(2,1)S(1)} %stack.21), channel_id=1, replica_groups=mesh['x'=4,'core'=2,'z'=8,'y'=4] {'y'}, dimensions={0} | all-to-all | bytes 4194304 | tf_op jit(solution)/shard_map/all_to_all | solution.py:38
  202.8 1.3 fusion.19
  204.2 4.0 %collective-permute-start.2 = (bf16[512,512]{1,0:T(8,128)(2,1)S(1)}, bf16[512,512]{1,0:T(8,128)(2,1)S(1)}, u32[]{:S(2)}, u32[]{:S(2)}) collective-permute-start(bf16[512,512]{1,0:T(8,128)(2,1)S(1)} %dynamic-slice_convert_fusion), channel_id=1, source_target_pairs={{0,32},{32,0},{1,33},{33,1},{2,34},{34,2},{3,35},{35,3},{4,36},{36... | collective-permute-start | bytes 1572872 | tf_op jit(solution)/shard_map/ppermute | solution.py:47
  208.2 1.5 collective-permute-done.2
  209.7 0.2 add_convert_fusion.1
  209.9 11.6 %all_to_all.100 = bf16[4,128,512]{2,1,0:T(8,128)(2,1)S(1)} all-to-all(bf16[4,128,512]{2,1,0:T(8,128)(2,1)S(1)} %bitcast.43), channel_id=1, replica_groups=mesh['x'=4,'core'=2,'z'=8,'y'=4] {'x'}, dimensions={0} | all-to-all | bytes 1048576 | tf_op jit(solution)/shard_map/all_to_all | solution.py:20
  222.2 16.4 %all_to_all.101 = bf16[4,128,1024]{2,1,0:T(8,128)(2,1)S(1)} all-to-all(bf16[4,128,1024]{2,1,0:T(8,128)(2,1)S(1)} %broadcast_in_dim.11), channel_id=1, replica_groups=mesh['x'=4,'core'=2,'z'=8,'y'=4] {'x'}, dimensions={0} | all-to-all | bytes 2097152 | tf_op jit(solution)/shard_map/all_to_all | solution.py:20
  238.6 2.1 collective-permute-start.3
  240.7 2.3 collective-permute-done.3
  243.0 0.2 broadcast_select_fusion.1
  243.2 1.3 fusion.10
  244.5 1.3 add_convert_fusion
  245.8 29.3 %all_to_all.102 = bf16[4,256,1024]{2,1,0:T(8,128)(2,1)} all-to-all(bf16[4,256,1024]{2,1,0:T(8,128)(2,1)S(1)} %bitcast.40), channel_id=1, replica_groups=mesh['x'=4,'core'=2,'z'=8,'y'=4] {'y'}, dimensions={0} | all-to-all | bytes 4194304 | tf_op jit(solution)/shard_map/all_to_all | solution.py:20
  275.1 3.0 reduce_sum.67
  278.0 4.1 %all-to-all-start.11 = ((bf16[8,32,1024]{2,1,0:T(8,128)(2,1)}), bf16[8,32,1024]{2,1,0:T(8,128)(2,1)}, u32[]{:S(2)}, u32[]{:S(2)}) async-start(bf16[8,32,1024]{2,1,0:T(8,128)(2,1)} %bitcast.50), calls=%async_computation.11 | async-start | bytes 1048576 | tf_op jit(solution)/shard_map/all_to_all | solution.py:20
  282.2 4.3 %convolution_convert_fusion.1 = bf16[512,1024]{1,0:T(8,128)(2,1)} fusion(bf16[1024,1024]{1,0:T(8,128)(2,1)} %bitcast.47, bf16[512,512]{1,0:T(8,128)(2,1)} %copy-done.12, bf16[512,512]{1,0:T(8,128)(2,1)} %copy-done.11), kind=kOutput, calls=%fused_computation.14 | convolution fusion | flops 1076363264 | bytes 4194304 | tf_op jit(solution)/shard_map/dot_general | solution.py:12
  286.5 2.2 fusion.6
  288.7 2.3 copy.33
  291.0 3.8 %fusion.5 = bf16[1024,512]{0,1:T(8,128)(2,1)} fusion(bf16[1024,1024]{1,0:T(8,128)(2,1)} %bitcast.37, bf16[512,1024]{1,0:T(8,128)(2,1)S(1)} %get-tuple-element.25, bf16[512,1024]{1,0:T(8,128)(2,1)S(1)} %get-tuple-element.26), kind=kOutput, calls=%fused_computation.17 | convolution fusion | flops 1076363264 | bytes 5242880 | tf_op jit(solution)/shard_map/dot_general | solution.py:12
  294.9 2.3 copy.32
  297.1 2.1 all-to-all-done.11
  299.2 1.8 reduce_sum.68
  (37 shorter events, 1.4 us)
Async XLA Ops:
  0.6 104.7 %copy-start = (bf16[512,1024]{1,0:T(8,128)(2,1)S(1)}, bf16[512,1024]{1,0:T(8,128)(2,1)}, u32[]{:S(2)}) copy-start(bf16[512,1024]{1,0:T(8,128)(2,1)} %param.9) | copy-start | bytes 3145732
  28.2 28.0 %all-to-all-start.1 = ((bf16[4,256,1024]{2,1,0:T(8,128)(2,1)}), bf16[4,256,1024]{2,1,0:T(8,128)(2,1)S(1)}, u32[]{:S(2)}, u32[]{:S(2)}) async-start(bf16[4,256,1024]{2,1,0:T(8,128)(2,1)} %stack.9), calls=%async_computation.1 | async-start | bytes 4194304 | tf_op jit(solution)/shard_map/all_to_all | solution.py:38
  56.2 1.3 copy-start.2
  57.5 3.3 %copy-start.3 = (bf16[4,256,1024]{2,1,0:T(8,128)(2,1)S(1)}, bf16[4,256,1024]{2,1,0:T(8,128)(2,1)}, u32[]{:S(2)}) copy-start(bf16[4,256,1024]{2,1,0:T(8,128)(2,1)} %copy-done.2) | copy-start | bytes 6291460
  57.5 3.3 %copy-start.9 = (bf16[1024,512]{1,0:T(8,128)(2,1)S(1)}, bf16[1024,512]{1,0:T(8,128)(2,1)}, u32[]{:S(2)}) copy-start(bf16[1024,512]{1,0:T(8,128)(2,1)} %param.7) | copy-start | bytes 3145732
  62.1 1.6 copy-start.1
  63.8 6.1 %collective-permute-start = (bf16[512,1024]{0,1:T(8,128)(2,1)}, bf16[512,1024]{0,1:T(8,128)(2,1)}, u32[]{:S(2)}, u32[]{:S(2)}) collective-permute-start(bf16[512,1024]{0,1:T(8,128)(2,1)} %fusion.1), channel_id=1, source_target_pairs={{0,32},{32,0},{1,33},{33,1},{2,34},{34,2},{3,35},{35,3},{4,36},{36... | collective-permute-start | bytes 3145736 | tf_op jit(solution)/shard_map/ppermute | solution.py:47
  89.8 0.8 copy-start.5
  101.0 4.2 %collective-permute-start.1 = (bf16[512,512]{1,0:T(8,128)(2,1)S(1)}, bf16[512,512]{1,0:T(8,128)(2,1)S(1)}, u32[]{:S(2)}, u32[]{:S(2)}) collective-permute-start(bf16[512,512]{1,0:T(8,128)(2,1)S(1)} %bitcast.42), channel_id=1, source_target_pairs={{0,32},{32,0},{1,33},{33,1},{2,34},{34,2},{3,35},{35,3},{4,36},{36... | collective-permute-start | bytes 1572872 | tf_op jit(solution)/shard_map/ppermute | solution.py:47
  105.4 1.3 copy-start.11
  105.4 1.3 copy-start.12
  136.5 20.5 %all-to-all-start.5 = ((bf16[8,32,1024]{2,1,0:T(8,128)(2,1)}), bf16[8,32,1024]{2,1,0:T(8,128)(2,1)S(1)}, u32[]{:S(2)}, u32[]{:S(2)}) async-start(bf16[8,32,1024]{2,1,0:T(8,128)(2,1)} %bitcast.49), calls=%async_computation.5 | async-start | bytes 1048576 | tf_op jit(solution)/shard_map/all_to_all | solution.py:20
  202.8 1.3 copy-start.7
  204.2 17.5 %copy-start.6 = (f32[128,1024]{0,1:T(8,128)S(1)}, f32[128,1024]{0,1:T(8,128)}, u32[]{:S(2)}) copy-start(f32[128,1024]{0,1:T(8,128)} %copy-done.5) | copy-start | bytes 1572868
  204.2 5.5 %collective-permute-start.2 = (bf16[512,512]{1,0:T(8,128)(2,1)S(1)}, bf16[512,512]{1,0:T(8,128)(2,1)S(1)}, u32[]{:S(2)}, u32[]{:S(2)}) collective-permute-start(bf16[512,512]{1,0:T(8,128)(2,1)S(1)} %dynamic-slice_convert_fusion), channel_id=1, source_target_pairs={{0,32},{32,0},{1,33},{33,1},{2,34},{34,2},{3,35},{35,3},{4,36},{36... | collective-permute-start | bytes 1572872 | tf_op jit(solution)/shard_map/ppermute | solution.py:47
  238.6 4.6 %copy-start.8 = (bf16[1024,512]{1,0:T(8,128)(2,1)S(1)}, bf16[1024,512]{1,0:T(8,128)(2,1)}, u32[]{:S(2)}) copy-start(bf16[1024,512]{1,0:T(8,128)(2,1)} %param.8) | copy-start | bytes 3145732
  238.6 4.4 %collective-permute-start.3 = (bf16[512,1024]{1,0:T(8,128)(2,1)S(1)}, bf16[512,1024]{1,0:T(8,128)(2,1)S(1)}, u32[]{:S(2)}, u32[]{:S(2)}) collective-permute-start(bf16[512,1024]{1,0:T(8,128)(2,1)S(1)} %bitcast.41), channel_id=1, source_target_pairs={{0,32},{32,0},{1,33},{33,1},{2,34},{34,2},{3,35},{35,3},{4,36},{36... | collective-permute-start | bytes 3145736 | tf_op jit(solution)/shard_map/ppermute | solution.py:47
  243.2 1.3 copy-start.10
  278.0 21.2 %all-to-all-start.11 = ((bf16[8,32,1024]{2,1,0:T(8,128)(2,1)}), bf16[8,32,1024]{2,1,0:T(8,128)(2,1)}, u32[]{:S(2)}, u32[]{:S(2)}) async-start(bf16[8,32,1024]{2,1,0:T(8,128)(2,1)} %bitcast.50), calls=%async_computation.11 | async-start | bytes 1048576 | tf_op jit(solution)/shard_map/all_to_all | solution.py:20
  282.2 4.3 %copy-start.4 = (bf16[4,256,1024]{2,1,0:T(8,128)(2,1)S(1)}, bf16[4,256,1024]{2,1,0:T(8,128)(2,1)}, u32[]{:S(2)}) copy-start(bf16[4,256,1024]{2,1,0:T(8,128)(2,1)} %copy-done.2) | copy-start | bytes 6291460
